TPU v7x, 32 devices: a whole 2x2x4 slice. The times are simulated.
32 devices in a mesh: nodes: 16 (over z, y, x), rep: 2 (over core).
Axes of the slice: x: 2, y: 2, z: 4, core: 2. Of those that a mesh axis runs over, the one named last changes fastest.
Arguments:
- node_latent: bfloat16 [5120, 512], P(('nodes', 'rep')), may hold values from -6 to 6
- edge_saved: bfloat16 [40960, 512], P(('nodes', 'rep')), may hold values from -6 to 6
- node_cot: bfloat16 [5120, 512], P(('nodes', 'rep')), may hold values from -6 to 6
- edge_cot: bfloat16 [40960, 512], P(('nodes', 'rep')), may hold values from -6 to 6
- senders: int32 [40960], P(('nodes', 'rep')), may hold values from 0 to 447, as said below
- receivers: int32 [40960], P(('nodes', 'rep')), may hold values from 0 to 319
- ghost_rows: int32 [16, 16, 8], P('nodes'), may hold values from 0 to 319, as said below
- w_edge_in: bfloat16 [1536, 512], replicated, may hold values from -0.15625 to 0.15625
- w_edge_out: bfloat16 [512, 512], replicated, may hold values from -0.25 to 0.25
- edge_gain: float32 [512], replicated, may hold values from 0.5 to 2
- edge_offset: float32 [512], replicated, may hold values from -3 to 3
- w_node_in: bfloat16 [1024, 512], replicated, may hold values from -0.1875 to 0.1875
- w_node_out: bfloat16 [512, 512], replicated, may hold values from -0.25 to 0.25
- node_gain: float32 [512], replicated, may hold values from 0.5 to 2
Outputs:
- grad_nodes: bfloat16 [5120, 512], P(('nodes', 'rep'))
- grad_edges: bfloat16 [40960, 512], P(('nodes', 'rep'))
- grad_edge_in: bfloat16 [1536, 512], replicated
- grad_edge_out: bfloat16 [512, 512], replicated
- grad_node_in: bfloat16 [1024, 512], replicated
- grad_node_out: bfloat16 [512, 512], replicated
Inputs may be any that keep to these rules, and one draw needn't show every extreme that they name: `senders`: A sender below 320 is a node of the edge's own partition; otherwise it is 320 + q * 8 + s, the ghost slot s of the list of a partition q other than the edge's own. Each list ghost_rows[q, p] holds 8 distinct rows.
All inputs are finite; a program needn't handle non-finite values.
Results may differ from a plain program's by a relative error of at most 0.008.
Values may be sent and summed in bfloat16 or wider, within the bound.
A program may use at most 128 MiB of HBM per device.

v0:
```python
import math
import jax
import jax.numpy as jnp
from jax import lax
from jax.sharding import PartitionSpec as P

EPS = 1e-05


def swapped(array, axis, bit):
    return lax.ppermute(array, axis, [(i, i ^ 1 << bit) for i in range(lax.axis_size(axis))])


def mat_mul(left, right):
    return jnp.dot(left, right, preferred_element_type=jnp.float32)


def mat_tn(left, right):
    return lax.dot_general(
        left, right, (((0,), (0,)), ((), ())), preferred_element_type=jnp.float32
    )


def mat_nt(left, right):
    return lax.dot_general(
        left, right, (((1,), (1,)), ((), ())), preferred_element_type=jnp.float32
    )


def silu_slope(value):
    sigmoid_v = jax.nn.sigmoid(value)
    return sigmoid_v * (1.0 + value * (1.0 - sigmoid_v))


def norm_forward(value):
    centred = value - jnp.mean(value, axis=-1, keepdims=True)
    inverse = lax.rsqrt(jnp.mean(centred * centred, axis=-1, keepdims=True) + EPS)
    return (centred * inverse, inverse)


def norm_backward(grad_hat, normed, inverse):
    return inverse * (
        grad_hat
        - jnp.mean(grad_hat, axis=-1, keepdims=True)
        - normed * jnp.mean(grad_hat * normed, axis=-1, keepdims=True)
    )


def edge_forward(edge_block, send_rows, recv_rows, w_edge_in, w_edge_out, edge_gain, edge_offset):
    latent_width = edge_block.shape[1]
    pre_act = (
        mat_mul(edge_block, w_edge_in[:latent_width])
        + mat_mul(send_rows, w_edge_in[latent_width : 2 * latent_width])
        + mat_mul(recv_rows, w_edge_in[2 * latent_width :])
    )
    edge_hidden = jax.nn.silu(pre_act).astype(jnp.bfloat16)
    edge_normed, edge_inverse = norm_forward(mat_mul(edge_hidden, w_edge_out))
    message = edge_normed * edge_gain + edge_offset
    return (pre_act, edge_hidden, edge_normed, edge_inverse, message)


def edge_backward(
    edge_block,
    send_rows,
    recv_rows,
    edge_cot,
    message_grad,
    saved,
    w_edge_in,
    w_edge_out,
    edge_gain,
):
    pre_act, edge_hidden, edge_normed, edge_inverse = saved
    latent_width = edge_block.shape[1]
    grad_out = norm_backward(message_grad * edge_gain, edge_normed, edge_inverse).astype(
        jnp.bfloat16
    )
    grad_act = (mat_nt(grad_out, w_edge_out) * silu_slope(pre_act)).astype(jnp.bfloat16)
    in_grad = jnp.concatenate(
        [mat_tn(edge_block, grad_act), mat_tn(send_rows, grad_act), mat_tn(recv_rows, grad_act)], 0
    )
    out_grad = mat_tn(edge_hidden, grad_out)
    edge_grad = (edge_cot.astype(jnp.float32) + mat_nt(grad_act, w_edge_in[:latent_width])).astype(
        jnp.bfloat16
    )
    send_grad = mat_nt(grad_act, w_edge_in[latent_width : 2 * latent_width])
    recv_grad = mat_nt(grad_act, w_edge_in[2 * latent_width :])
    return (edge_grad, send_grad, recv_grad, in_grad, out_grad)


def node_pass(node_rows, totals_b, node_cot, w_node_in, w_node_out, node_gain):
    latent_width = node_rows.shape[1]
    node_pre = mat_mul(node_rows, w_node_in[:latent_width]) + mat_mul(
        totals_b, w_node_in[latent_width:]
    )
    node_hidden = jax.nn.silu(node_pre).astype(jnp.bfloat16)
    node_normed, node_inverse = norm_forward(mat_mul(node_hidden, w_node_out))
    grad_out = norm_backward(
        node_cot.astype(jnp.float32) * node_gain, node_normed, node_inverse
    ).astype(jnp.bfloat16)
    grad_act = (mat_nt(grad_out, w_node_out) * silu_slope(node_pre)).astype(jnp.bfloat16)
    in_grad = jnp.concatenate([mat_tn(node_rows, grad_act), mat_tn(totals_b, grad_act)], 0)
    direct_grad = mat_nt(grad_act, w_node_in[:latent_width])
    totals_grad = mat_nt(grad_act, w_node_in[latent_width:]).astype(jnp.bfloat16)
    return (direct_grad, totals_grad, in_grad, mat_tn(node_hidden, grad_out))


def shards(
    node_latent,
    edge_saved,
    node_cot,
    edge_cot,
    senders,
    receivers,
    ghost_rows,
    w_edge_in,
    w_edge_out,
    edge_gain,
    edge_offset,
    w_node_in,
    w_node_out,
    node_gain,
):
    latent_width = node_latent.shape[1]
    edge_latent = swapped(edge_saved, "rep", 0)
    partition = lax.all_gather(node_latent, "rep", axis=0, tiled=True)
    part_rows = partition.shape[0]
    ghost_lists = ghost_rows[0]
    part_count = ghost_lists.shape[0]
    slot_count = ghost_lists.shape[1]
    outgoing = partition[ghost_lists.reshape(-1)].reshape(part_count, slot_count, latent_width)
    ghosts = lax.all_to_all(outgoing, "nodes", split_axis=0, concat_axis=0, tiled=True)
    node_table = jnp.concatenate(
        [partition, ghosts.reshape(part_count * slot_count, latent_width)], 0
    )
    send_rows = node_table[senders]
    recv_rows = partition[receivers]
    pre_act, edge_hidden, edge_normed, edge_inverse, message = edge_forward(
        edge_latent, send_rows, recv_rows, w_edge_in, w_edge_out, edge_gain, edge_offset
    )
    partial_totals = jax.ops.segment_sum(message, receivers, num_segments=part_rows)
    totals = lax.psum_scatter(partial_totals, "rep", scatter_dimension=0, tiled=True)
    direct_grad, totals_grad, node_in_grad, node_out_grad = node_pass(
        node_latent, totals.astype(jnp.bfloat16), node_cot, w_node_in, w_node_out, node_gain
    )
    partition_totals_grad = lax.all_gather(totals_grad, "rep", axis=0, tiled=True)
    message_grad = edge_cot.astype(jnp.float32) + partition_totals_grad[receivers].astype(
        jnp.float32
    )
    edge_grad, send_grad, recv_grad, edge_in_grad, edge_out_grad = edge_backward(
        edge_latent,
        send_rows,
        recv_rows,
        edge_cot,
        message_grad,
        (pre_act, edge_hidden, edge_normed, edge_inverse),
        w_edge_in,
        w_edge_out,
        edge_gain,
    )
    table_grad = jax.ops.segment_sum(send_grad, senders, num_segments=node_table.shape[0])
    row_grad = table_grad[:part_rows] + jax.ops.segment_sum(
        recv_grad, receivers, num_segments=part_rows
    )
    ghost_grad = table_grad[part_rows:].reshape(part_count, slot_count, latent_width)
    returned = lax.all_to_all(
        ghost_grad.astype(jnp.bfloat16), "nodes", split_axis=0, concat_axis=0, tiled=True
    ).astype(ghost_grad.dtype)
    row_grad = row_grad + jax.ops.segment_sum(
        returned.reshape(-1, latent_width), ghost_lists.reshape(-1), num_segments=part_rows
    )
    own_grad = lax.psum_scatter(row_grad, "rep", scatter_dimension=0, tiled=True)
    grad_nodes = (own_grad + direct_grad + node_cot.astype(jnp.float32)).astype(jnp.bfloat16)
    weight_grads = (edge_in_grad, edge_out_grad, node_in_grad, node_out_grad)
    device_count = lax.axis_size("nodes") * lax.axis_size("rep")
    edge_scale = 1.0 / math.sqrt(senders.shape[0] * device_count)
    node_scale = 1.0 / math.sqrt(node_latent.shape[0] * device_count)
    weight_total = lax.psum(
        (weight_grads[0], weight_grads[1], weight_grads[2], weight_grads[3]), ("nodes", "rep")
    )
    return (
        grad_nodes,
        edge_grad,
        (weight_total[0] * edge_scale).astype(jnp.bfloat16),
        (weight_total[1] * edge_scale).astype(jnp.bfloat16),
        (weight_total[2] * node_scale).astype(jnp.bfloat16),
        (weight_total[3] * node_scale).astype(jnp.bfloat16),
    )


def solution(mesh):
    return jax.shard_map(
        shards,
        mesh=mesh,
        in_specs=(
            P(("nodes", "rep"), None),
            P(("nodes", "rep"), None),
            P(("nodes", "rep"), None),
            P(("nodes", "rep"), None),
            P(("nodes", "rep")),
            P(("nodes", "rep")),
            P("nodes", None, None),
            P(),
            P(),
            P(),
            P(),
            P(),
            P(),
            P(),
        ),
        out_specs=(P(("nodes", "rep"), None), P(("nodes", "rep"), None), P(), P(), P(), P()),
        check_vma=False,
    )
```

profile of v0, /device:TPU:0, one launch (start us, length us, event | category | flops | bytes accessed | tf_op | source)
XLA Modules:
  0.0 329.2 jit_solution(6399339282677917739)
XLA Ops:
  7.2 2.5 all_gather.6
  12.1 8.2 %all-to-all-start = ((bf16[16,8,512]{2,1,0:T(8,128)(2,1)}), bf16[16,8,512]{2,1,0:T(8,128)(2,1)S(1)}, u32[]{:S(2)}, u32[]{:S(2)}) async-start(bf16[16,8,512]{2,1,0:T(8,128)(2,1)} %bitcast.1), calls=%async_computation | async-start | bytes 262144 | tf_op jit(solution)/shard_map/all_to_all | solution.py:132
  21.1 4.1 %gather_fusion.2 = bf16[1280,512]{1,0:T(8,128)(2,1)S(1)} fusion(bf16[320,512]{1,0:T(8,128)(2,1)S(1)} %all_gather.6, s32[2048]{0:T(1024)S(1)} %pad_clamp_fusion), kind=kCustom, calls=%fused_computation.2 | custom fusion | bytes 2626560 | tf_op jit(solution)/shard_map/gather | solution.py:137
  25.3 3.8 %fusion.15 = f32[1280,512]{1,0:T(8,128)} fusion(bf16[1280,512]{1,0:T(8,128)(2,1)S(1)} %gather_fusion.2, bf16[1536,512]{1,0:T(8,128)(2,1)} %param.21), kind=kOutput, calls=%fused_computation.46 | convolution fusion | flops 671088640 | bytes 4456448 | tf_op jit(solution)/shard_map/dot_general | solution.py:15
  29.1 4.1 %gather_fusion.1 = bf16[1280,512]{1,0:T(8,128)(2,1)S(1)} fusion(bf16[448,512]{1,0:T(8,128)(2,1)S(1)} %pad_maximum_fusion.2, s32[2048]{0:T(1024)S(1)} %pad_clamp_fusion.1), kind=kCustom, calls=%fused_computation.1 | custom fusion | bytes 2626560 | tf_op jit(solution)/shard_map/gather | solution.py:136
  33.2 2.4 fusion.19
  35.7 4.2 %multiply_convert_fusion.2 = (bf16[1280,512]{1,0:T(8,128)(2,1)S(1)}, f32[1280,512]{1,0:T(8,128)}) fusion(f32[1280,512]{1,0:T(8,128)S(1)} %copy-done.12, f32[1280,512]{1,0:T(8,128)S(1)} %fusion.19, bf16[1280,512]{1,0:T(8,128)(2,1)} %collective-permute-done, bf16[1536,512]{1,0:T(8,128)(2,1)} %param.21), kind=kOutput, calls=%fused_computation.22 | convolution fusion | flops 675676160 | bytes 11010048 | tf_op jit(solution)/shard_map/dot_general | solution.py:15
  41.7 1.9 multiply_add_fusion
  43.6 3.2 copy.28
  46.9 11.1 %scatter_custom_fusion = f32[320,512]{1,0:T(8,128)} fusion(s32[1280]{0:T(1024)S(1)} %copy-done.34, f32[1280,512]{1,0:T(8,128)} %copy.28, f32[]{:T(128)} %constant.10.clone.1), kind=kCustom, calls=%fused_computation.70 | custom fusion | flops 655360 | bytes 655872 | tf_op jit(solution)/shard_map/scatter-add | solution.py:141
  58.1 2.4 copy.27
  60.5 2.0 fusion.11
  62.5 5.1 %reduce-scatter.3.cloned.1.call-done = f32[160,512]{1,0:T(8,128)} async-done(((f32[320,512]{1,0:T(8,128)}), f32[160,512]{1,0:T(8,128)}) %reduce-scatter.3.cloned.1.call-update) | async-done | bytes 327696 | tf_op jit(solution)/shard_map/reduce_scatter | solution.py:142
  72.7 2.2 all_gather.7
  74.9 4.7 %gather_fusion.3 = bf16[1280,512]{1,0:T(8,128)(2,1)} fusion(bf16[320,512]{1,0:T(8,128)(2,1)S(1)} %all_gather.7, s32[2048]{0:T(1024)S(1)} %pad_clamp_fusion), kind=kCustom, calls=%fused_computation.3 | custom fusion | bytes 2626560 | tf_op jit(solution)/shard_map/gather | solution.py:147
  79.6 2.4 copy.29
  82.1 2.7 fusion.4
  88.0 2.4 fusion.17
  90.5 2.4 fusion.13
  92.8 10.6 %scatter_custom_fusion.1 = f32[448,512]{1,0:T(8,128)S(1)} fusion(s32[1280]{0:T(1024)S(1)} %copy-done.36, f32[1280,512]{1,0:T(8,128)} %fusion.17, f32[]{:T(128)} %constant.10.clone.1), kind=kCustom, calls=%fused_computation.55 | custom fusion | flops 655360 | bytes 918016 | tf_op jit(solution)/shard_map/scatter-add | solution.py:161
  104.1 3.2 fusion.50
  108.8 6.7 %all-to-all-start.1 = ((bf16[16,8,512]{2,1,0:T(8,128)(2,1)}), bf16[16,8,512]{2,1,0:T(8,128)(2,1)S(1)}, u32[]{:S(2)}, u32[]{:S(2)}) async-start(bf16[16,8,512]{2,1,0:T(8,128)(2,1)} %fusion.37), calls=%async_computation.2 | async-start | bytes 262144 | tf_op jit(solution)/shard_map/all_to_all | solution.py:166
  115.7 10.7 %scatter_fusion = f32[320,512]{1,0:T(8,128)S(1)} fusion(f32[320,512]{1,0:T(8,128)S(1)} %slice.42, s32[1280]{0:T(1024)S(1)} %copy-done.34, f32[1280,512]{1,0:T(8,128)} %fusion.13), kind=kCustom, calls=%fused_computation.6 | custom fusion | flops 655360 | bytes 7869440 | tf_op jit(solution)/shard_map/scatter-add | solution.py:162
  131.7 3.2 pad_maximum_fusion.1
  136.6 1.9 fusion.51
  138.5 2.3 convolution_bitcast_fusion
  140.8 2.0 pad_maximum_fusion
  144.1 3.0 fusion.1
  147.1 2.5 copy.32
  149.6 2.0 fusion.7
  151.6 164.3 %all-reduce.3.cloned.1.call-done = (f32[1536,512]{1,0:T(8,128)}, f32[512,512]{1,0:T(8,128)}, f32[1024,512]{1,0:T(8,128)}, f32[512,512]{1,0:T(8,128)}) async-done(((f32[1536,512]{1,0:T(8,128)}, f32[512,512]{1,0:T(8,128)}, f32[1024,512]{1,0:T(8,128)}, f32[512,512]{1,0:T(8,128)}), (f32[1536,512]{1,0:T(8,128)}, f32[512,512]{1,0:T(8,128)}, f32[1024,512]{1,0:T(8,128)}, ...) | async-done | bytes 7340048 | tf_op jit(solution)/shard_map/psum | solution.py:178
  315.9 3.6 %multiply_convert_fusion = bf16[1536,512]{1,0:T(8,128)(2,1)} fusion(f32[1536,512]{1,0:T(8,128)} %get-tuple-element.22), kind=kLoop, calls=%fused_computation.14 | loop fusion | flops 1572864 | bytes 4718592 | tf_op jit(solution)/shard_map/convert_element_type | solution.py:184
  (132 shorter events, 27.0 us)
Async XLA Ops:
  7.2 32.7 %copy-start = (bf16[512,512]{1,0:T(8,128)(2,1)S(1)}, bf16[512,512]{1,0:T(8,128)(2,1)}, u32[]{:S(2)}) copy-start(bf16[512,512]{1,0:T(8,128)(2,1)} %param.22) | copy-start | bytes 1572868
  12.1 17.0 %all-to-all-start = ((bf16[16,8,512]{2,1,0:T(8,128)(2,1)}), bf16[16,8,512]{2,1,0:T(8,128)(2,1)S(1)}, u32[]{:S(2)}, u32[]{:S(2)}) async-start(bf16[16,8,512]{2,1,0:T(8,128)(2,1)} %bitcast.1), calls=%async_computation | async-start | bytes 262144 | tf_op jit(solution)/shard_map/all_to_all | solution.py:132
  20.3 47.3 %reduce-scatter.3.cloned.1.call-start = ((), (), s32[]{:S(2)}) async-start(), calls=%async_computation.4 | async-start | bytes 983040 | tf_op jit(solution)/shard_map/reduce_scatter | solution.py:142
  20.3 15.3 %collective-permute-start = (bf16[1280,512]{1,0:T(8,128)(2,1)}, bf16[1280,512]{1,0:T(8,128)(2,1)}, u32[]{:S(2)}, u32[]{:S(2)}) collective-permute-start(bf16[1280,512]{1,0:T(8,128)(2,1)} %param.15), channel_id=1, source_target_pairs={{0,1},{1,0},{2,3},{3,2},{4,5},{5,4},{6,7},{7,6},{8,9},{9,8},{10,11... | collective-permute-start | bytes 3932168 | tf_op jit(solution)/shard_map/ppermute | solution.py:11
  21.1 4.1 %copy-start.36 = (s32[1280]{0:T(1024)S(1)}, s32[1280]{0:T(1024)}, u32[]{:S(2)}) copy-start(s32[1280]{0:T(1024)} %param.18) | copy-start | bytes 15364
  25.3 3.8 %copy-start.7 = (bf16[1280,512]{1,0:T(8,128)(2,1)}, bf16[1280,512]{1,0:T(8,128)(2,1)S(1)}, u32[]{:S(2)}) copy-start(bf16[1280,512]{1,0:T(8,128)(2,1)S(1)} %gather_fusion.2) | copy-start | bytes 3932164
  33.2 2.4 copy-start.5
  33.2 2.4 copy-start.12
  43.6 3.2 copy-start.34
  46.8 13.6 %copy-start.16 = (bf16[160,512]{1,0:T(8,128)(2,1)S(1)}, bf16[160,512]{1,0:T(8,128)(2,1)}, u32[]{:S(2)}) copy-start(bf16[160,512]{1,0:T(8,128)(2,1)} %param.14) | copy-start | bytes 491524
  62.5 8.4 %copy-start.30 = (bf16[160,512]{1,0:T(8,128)(2,1)S(1)}, bf16[160,512]{1,0:T(8,128)(2,1)}, u32[]{:S(2)}) copy-start(bf16[160,512]{1,0:T(8,128)(2,1)} %param.16) | copy-start | bytes 491524
  62.5 8.4 %copy-start.38 = (f32[512]{0:T(512)S(1)}, f32[512]{0:T(512)}, u32[]{:S(2)}) copy-start(f32[512]{0:T(512)} %param.27) | copy-start | bytes 6148
  67.6 3.6 %copy-start.39 = (bf16[512,512]{1,0:T(8,128)(2,1)S(1)}, bf16[512,512]{1,0:T(8,128)(2,1)}, u32[]{:S(2)}) copy-start(bf16[512,512]{1,0:T(8,128)(2,1)} %param.26) | copy-start | bytes 1572868
  69.1 2.4 copy-start.32
  82.0 2.7 copy-start.2
  82.0 2.7 copy-start.4
  88.0 2.4 copy-start.9
  92.8 11.3 %copy-start.8 = (bf16[1280,512]{1,0:T(8,128)(2,1)S(1)}, bf16[1280,512]{1,0:T(8,128)(2,1)}, u32[]{:S(2)}) copy-start(bf16[1280,512]{1,0:T(8,128)(2,1)} %copy-done.7) | copy-start | bytes 3932164
  104.1 3.2 copy-start.21
  104.1 3.2 copy-start.31
  104.1 3.2 copy-start.33
  108.8 20.3 %all-to-all-start.1 = ((bf16[16,8,512]{2,1,0:T(8,128)(2,1)}), bf16[16,8,512]{2,1,0:T(8,128)(2,1)S(1)}, u32[]{:S(2)}, u32[]{:S(2)}) async-start(bf16[16,8,512]{2,1,0:T(8,128)(2,1)} %fusion.37), calls=%async_computation.2 | async-start | bytes 262144 | tf_op jit(solution)/shard_map/all_to_all | solution.py:166
  115.6 10.8 %copy-start.19 = (bf16[160,512]{1,0:T(8,128)(2,1)S(1)}, bf16[160,512]{1,0:T(8,128)(2,1)}, u32[]{:S(2)}) copy-start(bf16[160,512]{1,0:T(8,128)(2,1)} %copy-done.18) | copy-start | bytes 491524
  115.6 10.8 %copy-start.26 = (f32[160,512]{1,0:T(8,128)S(1)}, f32[160,512]{1,0:T(8,128)}, u32[]{:S(2)}) copy-start(f32[160,512]{1,0:T(8,128)} %reduce-scatter.3.cloned.1.call-done) | copy-start | bytes 983044
  115.6 12.2 %copy-start.17 = (bf16[160,512]{1,0:T(8,128)(2,1)S(1)}, bf16[160,512]{1,0:T(8,128)(2,1)}, u32[]{:S(2)}) copy-start(bf16[160,512]{1,0:T(8,128)(2,1)} %param.14) | copy-start | bytes 491524
  115.6 34.0 %reduce-scatter.5.cloned.1.call-start = ((), (), s32[]{:S(2)}) async-start(), calls=%async_computation.5 | async-start | bytes 983040 | tf_op jit(solution)/shard_map/reduce_scatter | solution.py:172
  131.6 3.3 %copy-start.6 = (bf16[1280,512]{1,0:T(8,128)(2,1)S(1)}, bf16[1280,512]{1,0:T(8,128)(2,1)}, u32[]{:S(2)}) copy-start(bf16[1280,512]{1,0:T(8,128)(2,1)} %copy-done.5) | copy-start | bytes 3932164
  131.6 3.3 copy-start.10
  131.6 184.3 %all-reduce.3.cloned.1.call-start = ((), (), s32[]{:S(2)}) async-start(), calls=%async_computation.6 | async-start | bytes 14680064 | tf_op jit(solution)/shard_map/psum | solution.py:178
  147.1 2.5 copy-start.14
  315.9 3.6 %copy-start.28 = (f32[512,512]{1,0:T(8,128)S(1)}, f32[512,512]{1,0:T(8,128)}, u32[]{:S(2)}) copy-start(f32[512,512]{1,0:T(8,128)} %get-tuple-element.23) | copy-start | bytes 3145732
  315.9 4.6 %copy-start.15 = (f32[1024,512]{1,0:T(8,128)S(1)}, f32[1024,512]{1,0:T(8,128)}, u32[]{:S(2)}) copy-start(f32[1024,512]{1,0:T(8,128)} %get-tuple-element.24) | copy-start | bytes 6291460
  (15 other events, 22.7 us)
Sparse Core Ops, SparseCore 0:
  58.1 9.4 reduce-scatter.2
  131.7 9.3 reduce-scatter.4
  147.3 168.5 all-reduce.2
where the time goes:
time: 330 us; the launch traced here: 329 us
  waiting for transfers between devices  169 us (51%)
  other arithmetic  53.9 us (16%)
  matrix products  40.7 us (12%)
  local copies, waits for them, and re-layouts  31 us (9%)
  starting transfers between devices  15.1 us (5%)
  between operations  14.3 us (4%)
  blocking collectives  4.72 us (1%)
    psum x1, waiting for transfers between devices, shards(): lax.psum((weight_grads[0], weight_grads[1], weight_grads[2], weight_grads...  164 us
    dot_general x7, matrix products, mat_mul(): return jnp.dot(left, right, preferred_element_type=jnp.float32)  16.4 us
    dot_general x7, matrix products, mat_tn(): lax.dot_general(left, right, (((0,), (0,)), ((), ())), preferred_element_...  12.4 us
    dot_general x7, matrix products, mat_nt(): lax.dot_general(left, right, (((1,), (1,)), ((), ())), preferred_element_...  11.9 us
    scatter-add x1, other arithmetic, shards(): jax.ops.segment_sum(message, receivers, num_segments=part_rows)  11.1 us
    scatter-add x1, other arithmetic, shards(): jax.ops.segment_sum(recv_grad, receivers, num_segments=part_rows)  10.7 us
    scatter-add x1, other arithmetic, shards(): jax.ops.segment_sum(send_grad, senders, num_segments=node_table.shape[0])  10.6 us
    unnamed x85, local copies, waits for them, and re-layouts  10.1 us
  transfers between devices with their start and end apart: 6, of which 2 were waited for; matrix products, arithmetic and copies ran while one was open for 15% of the time, Pallas kernels for 0%

commit v1 on v0

--- a/solution.py
+++ b/solution.py
@@ -175,9 +175,9 @@
     device_count = lax.axis_size("nodes") * lax.axis_size("rep")
     edge_scale = 1.0 / math.sqrt(senders.shape[0] * device_count)
     node_scale = 1.0 / math.sqrt(node_latent.shape[0] * device_count)
-    weight_total = lax.psum(
-        (weight_grads[0], weight_grads[1], weight_grads[2], weight_grads[3]), ("nodes", "rep")
-    )
+    weight_total = (weight_grads[0], weight_grads[1], weight_grads[2], weight_grads[3])
+    for mesh_axis in ("nodes", "rep"):
+        weight_total = lax.psum(weight_total, mesh_axis)
     return (
         grad_nodes,
         edge_grad,

time: 330 us -> 399 us (1.21)
  waiting for transfers between devices: 169 us -> 239 us
    psum x1 -> x2, waiting for transfers between devices: 164 us -> 232 us  [shards(): weight_total = lax.psum(weight_total, mesh_axis)]
    dot_general x7, matrix products: 12.4 us -> 7.91 us  [mat_tn(): lax.dot_general(left, right, (((0,), (0,)), ((), ())), preferred_element_...]
    unnamed x85 -> x73, local copies, waits for them, and re-layouts: 10.1 us -> 10.2 us
  transfers between devices with their start and end apart: 6 -> 7, of which waited for: 2 -> 4; matrix products, arithmetic and copies ran while one was open for 15% -> 15% of each run, Pallas kernels for 0% -> 0%
where the time goes in v1:
time: 399 us; the launch traced here: 398 us
  waiting for transfers between devices  239 us (60%)
  other arithmetic  53 us (13%)
  matrix products  38.2 us (10%)
  local copies, waits for them, and re-layouts  33.2 us (8%)
  starting transfers between devices  15.2 us (4%)
  between operations  14.2 us (4%)
  blocking collectives  4.72 us (1%)
    psum x2, waiting for transfers between devices, shards(): weight_total = lax.psum(weight_total, mesh_axis)  232 us
    dot_general x7, matrix products, mat_mul(): return jnp.dot(left, right, preferred_element_type=jnp.float32)  16.4 us
    dot_general x7, matrix products, mat_nt(): lax.dot_general(left, right, (((1,), (1,)), ((), ())), preferred_element_...  13.9 us
    scatter-add x1, other arithmetic, shards(): jax.ops.segment_sum(send_grad, senders, num_segments=node_table.shape[0])  11.4 us
    scatter-add x1, other arithmetic, shards(): jax.ops.segment_sum(message, receivers, num_segments=part_rows)  11.1 us
    scatter-add x1, other arithmetic, shards(): jax.ops.segment_sum(recv_grad, receivers, num_segments=part_rows)  10.6 us
    unnamed x73, local copies, waits for them, and re-layouts  10.2 us
    all_to_all x1, starting transfers between devices, shards(): lax.all_to_all(outgoing, 'nodes', split_axis=0, concat_axis=0, tiled=True)  8.22 us
  transfers between devices with their start and end apart: 7, of which 4 were waited for; matrix products, arithmetic and copies ran while one was open for 15% of the time, Pallas kernels for 0%

profile of v1, /device:TPU:0, one launch (start us, length us, event | category | flops | bytes accessed | tf_op | source)
XLA Modules:
  0.0 398.0 jit_solution(6100553544853896985)
XLA Ops:
  7.2 2.5 all_gather.6
  12.1 8.2 %all-to-all-start = ((bf16[16,8,512]{2,1,0:T(8,128)(2,1)}), bf16[16,8,512]{2,1,0:T(8,128)(2,1)S(1)}, u32[]{:S(2)}, u32[]{:S(2)}) async-start(bf16[16,8,512]{2,1,0:T(8,128)(2,1)} %bitcast.1), calls=%async_computation | async-start | bytes 262144 | tf_op jit(solution)/shard_map/all_to_all | solution.py:132
  21.1 4.1 %gather_fusion.2 = bf16[1280,512]{1,0:T(8,128)(2,1)S(1)} fusion(bf16[320,512]{1,0:T(8,128)(2,1)S(1)} %all_gather.6, s32[2048]{0:T(1024)S(1)} %pad_clamp_fusion), kind=kCustom, calls=%fused_computation.2 | custom fusion | bytes 2626560 | tf_op jit(solution)/shard_map/gather | solution.py:137
  25.3 3.7 fusion.15
  29.1 4.1 %gather_fusion.1 = bf16[1280,512]{1,0:T(8,128)(2,1)S(1)} fusion(bf16[448,512]{1,0:T(8,128)(2,1)S(1)} %pad_maximum_fusion.2, s32[2048]{0:T(1024)S(1)} %pad_clamp_fusion.1), kind=kCustom, calls=%fused_computation.1 | custom fusion | bytes 2626560 | tf_op jit(solution)/shard_map/gather | solution.py:136
  33.2 2.4 fusion.19
  35.6 4.3 %multiply_convert_fusion.2 = (bf16[1280,512]{1,0:T(8,128)(2,1)S(1)}, f32[1280,512]{1,0:T(8,128)}) fusion(f32[1280,512]{1,0:T(8,128)S(1)} %copy-done.9, f32[1280,512]{1,0:T(8,128)S(1)} %fusion.19, bf16[1280,512]{1,0:T(8,128)(2,1)} %collective-permute-done, bf16[1536,512]{1,0:T(8,128)(2,1)} %param.21), kind=kOutput, calls=%fused_computation.22 | convolution fusion | flops 675676160 | bytes 11010048 | tf_op jit(solution)/shard_map/dot_general | solution.py:15
  41.7 1.9 multiply_add_fusion
  43.6 3.3 copy.28
  47.0 11.1 %scatter_custom_fusion = f32[320,512]{1,0:T(8,128)} fusion(s32[1280]{0:T(1024)S(1)} %copy-done.28, f32[1280,512]{1,0:T(8,128)} %copy.28, f32[]{:T(128)} %constant.10.clone.1), kind=kCustom, calls=%fused_computation.70 | custom fusion | flops 655360 | bytes 655872 | tf_op jit(solution)/shard_map/scatter-add | solution.py:141
  58.1 2.4 copy.27
  60.6 2.0 fusion.11
  62.6 5.1 %reduce-scatter.3.cloned.1.call-done = f32[160,512]{1,0:T(8,128)} async-done(((f32[320,512]{1,0:T(8,128)}), f32[160,512]{1,0:T(8,128)}) %reduce-scatter.3.cloned.1.call-update) | async-done | bytes 327696 | tf_op jit(solution)/shard_map/reduce_scatter | solution.py:142
  72.8 2.2 all_gather.7
  75.0 4.7 %gather_fusion.3 = bf16[1280,512]{1,0:T(8,128)(2,1)} fusion(bf16[320,512]{1,0:T(8,128)(2,1)S(1)} %all_gather.7, s32[2048]{0:T(1024)S(1)} %pad_clamp_fusion), kind=kCustom, calls=%fused_computation.3 | custom fusion | bytes 2626560 | tf_op jit(solution)/shard_map/gather | solution.py:147
  79.7 2.4 copy.29
  82.2 2.7 fusion.4
  90.8 1.9 fusion.51
  96.4 2.2 convolution_bitcast_fusion
  98.6 2.1 pad_maximum_fusion
  100.7 3.4 fusion.17
  104.2 11.4 %scatter_custom_fusion.1 = f32[448,512]{1,0:T(8,128)} fusion(s32[1280]{0:T(1024)S(1)} %copy-done.30, f32[1280,512]{1,0:T(8,128)} %fusion.17, f32[]{:T(128)} %constant.10.clone.1), kind=kCustom, calls=%fused_computation.55 | custom fusion | flops 655360 | bytes 918016 | tf_op jit(solution)/shard_map/scatter-add | solution.py:161
  118.3 6.7 %all-to-all-start.1 = ((bf16[16,8,512]{2,1,0:T(8,128)(2,1)}), bf16[16,8,512]{2,1,0:T(8,128)(2,1)S(1)}, u32[]{:S(2)}, u32[]{:S(2)}) async-start(bf16[16,8,512]{2,1,0:T(8,128)(2,1)} %fusion.37), calls=%async_computation.2 | async-start | bytes 262144 | tf_op jit(solution)/shard_map/all_to_all | solution.py:166
  125.1 3.4 fusion.13
  128.5 10.6 %scatter_fusion = f32[320,512]{1,0:T(8,128)S(1)} fusion(f32[320,512]{1,0:T(8,128)S(1)} %slice.42, s32[1280]{0:T(1024)S(1)} %copy-done.28, f32[1280,512]{1,0:T(8,128)} %fusion.13), kind=kCustom, calls=%fused_computation.6 | custom fusion | flops 655360 | bytes 7869440 | tf_op jit(solution)/shard_map/scatter-add | solution.py:162
  141.7 195.5 %all-reduce.5.cloned.1.call-done = (f32[1536,512]{1,0:T(8,128)}, f32[512,512]{1,0:T(8,128)}, f32[1024,512]{1,0:T(8,128)}, f32[512,512]{1,0:T(8,128)}) async-done(((f32[1536,512]{1,0:T(8,128)}, f32[512,512]{1,0:T(8,128)}, f32[1024,512]{1,0:T(8,128)}, f32[512,512]{1,0:T(8,128)}), (f32[1536,512]{1,0:T(8,128)}, f32[512,512]{1,0:T(8,128)}, f32[1024,512]{1,0:T(8,128)}, ...) | async-done | bytes 7340048 | tf_op jit(solution)/shard_map/psum | solution.py:180
  338.5 3.0 fusion.1
  341.5 2.5 copy.32
  344.0 2.5 reduce-scatter.5.cloned.1.call-done
  346.5 2.0 fusion.7
  348.4 36.3 %all-reduce.7.cloned.1.call-done = (f32[1536,512]{1,0:T(8,128)}, f32[512,512]{1,0:T(8,128)}, f32[1024,512]{1,0:T(8,128)}, f32[512,512]{1,0:T(8,128)}) async-done(((f32[1536,512]{1,0:T(8,128)}, f32[512,512]{1,0:T(8,128)}, f32[1024,512]{1,0:T(8,128)}, f32[512,512]{1,0:T(8,128)}), (f32[1536,512]{1,0:T(8,128)}, f32[512,512]{1,0:T(8,128)}, f32[1024,512]{1,0:T(8,128)}, ...) | async-done | bytes 7340048 | tf_op jit(solution)/shard_map/psum | solution.py:180
  384.7 3.6 multiply_convert_fusion
  (123 shorter events, 29.6 us)
Async XLA Ops:
  7.2 32.8 %copy-start = (bf16[512,512]{1,0:T(8,128)(2,1)S(1)}, bf16[512,512]{1,0:T(8,128)(2,1)}, u32[]{:S(2)}) copy-start(bf16[512,512]{1,0:T(8,128)(2,1)} %param.22) | copy-start | bytes 1572868
  12.1 17.0 %all-to-all-start = ((bf16[16,8,512]{2,1,0:T(8,128)(2,1)}), bf16[16,8,512]{2,1,0:T(8,128)(2,1)S(1)}, u32[]{:S(2)}, u32[]{:S(2)}) async-start(bf16[16,8,512]{2,1,0:T(8,128)(2,1)} %bitcast.1), calls=%async_computation | async-start | bytes 262144 | tf_op jit(solution)/shard_map/all_to_all | solution.py:132
  20.3 47.4 %reduce-scatter.3.cloned.1.call-start = ((), (), s32[]{:S(2)}) async-start(), calls=%async_computation.4 | async-start | bytes 983040 | tf_op jit(solution)/shard_map/reduce_scatter | solution.py:142
  20.3 15.3 %collective-permute-start = (bf16[1280,512]{1,0:T(8,128)(2,1)}, bf16[1280,512]{1,0:T(8,128)(2,1)}, u32[]{:S(2)}, u32[]{:S(2)}) collective-permute-start(bf16[1280,512]{1,0:T(8,128)(2,1)} %param.15), channel_id=1, source_target_pairs={{0,1},{1,0},{2,3},{3,2},{4,5},{5,4},{6,7},{7,6},{8,9},{9,8},{10,11... | collective-permute-start | bytes 3932168 | tf_op jit(solution)/shard_map/ppermute | solution.py:11
  21.1 4.1 %copy-start.30 = (s32[1280]{0:T(1024)S(1)}, s32[1280]{0:T(1024)}, u32[]{:S(2)}) copy-start(s32[1280]{0:T(1024)} %param.18) | copy-start | bytes 15364
  25.3 3.8 copy-start.5
  33.2 2.4 copy-start.7
  33.2 2.4 copy-start.9
  43.6 3.3 copy-start.28
  47.0 13.6 %copy-start.13 = (bf16[160,512]{1,0:T(8,128)(2,1)S(1)}, bf16[160,512]{1,0:T(8,128)(2,1)}, u32[]{:S(2)}) copy-start(bf16[160,512]{1,0:T(8,128)(2,1)} %param.14) | copy-start | bytes 491524
  58.1 279.1 %all-reduce.5.cloned.1.call-start = ((), (), s32[]{:S(2)}) async-start(), calls=%async_computation.6 | async-start | bytes 14680064 | tf_op jit(solution)/shard_map/psum | solution.py:180
  62.6 8.4 %copy-start.24 = (bf16[160,512]{1,0:T(8,128)(2,1)S(1)}, bf16[160,512]{1,0:T(8,128)(2,1)}, u32[]{:S(2)}) copy-start(bf16[160,512]{1,0:T(8,128)(2,1)} %param.16) | copy-start | bytes 491524
  62.6 8.4 %copy-start.32 = (f32[512]{0:T(512)S(1)}, f32[512]{0:T(512)}, u32[]{:S(2)}) copy-start(f32[512]{0:T(512)} %param.27) | copy-start | bytes 6148
  67.7 3.6 copy-start.33
  69.2 2.4 copy-start.26
  82.2 2.7 copy-start.2
  82.2 2.7 copy-start.4
  84.9 1.7 copy-start.34
  90.8 1.9 copy-start.14
  90.8 1.9 copy-start.16
  90.8 2.3 copy-start.18
  90.8 2.3 copy-start.25
  90.8 2.3 copy-start.27
  92.7 1.8 copy-start.21
  118.3 20.8 %all-to-all-start.1 = ((bf16[16,8,512]{2,1,0:T(8,128)(2,1)}), bf16[16,8,512]{2,1,0:T(8,128)(2,1)S(1)}, u32[]{:S(2)}, u32[]{:S(2)}) async-start(bf16[16,8,512]{2,1,0:T(8,128)(2,1)} %fusion.37), calls=%async_computation.2 | async-start | bytes 262144 | tf_op jit(solution)/shard_map/all_to_all | solution.py:166
  125.1 221.4 %reduce-scatter.5.cloned.1.call-start = ((), (), s32[]{:S(2)}) async-start(), calls=%async_computation.5 | async-start | bytes 983040 | tf_op jit(solution)/shard_map/reduce_scatter | solution.py:172
  141.6 243.1 %all-reduce.7.cloned.1.call-start = ((), (), s32[]{:S(2)}) async-start(), calls=%async_computation.7 | async-start | bytes 14680064 | tf_op jit(solution)/shard_map/psum | solution.py:180
  341.5 5.0 %copy-start.11 = (bf16[1024,512]{1,0:T(8,128)(2,1)S(1)}, bf16[1024,512]{1,0:T(8,128)(2,1)}, u32[]{:S(2)}) copy-start(bf16[1024,512]{1,0:T(8,128)(2,1)} %param.25) | copy-start | bytes 3145732
  384.7 3.6 copy-start.23
  384.7 4.6 %copy-start.12 = (f32[1024,512]{1,0:T(8,128)S(1)}, f32[1024,512]{1,0:T(8,128)}, u32[]{:S(2)}) copy-start(f32[1024,512]{1,0:T(8,128)} %get-tuple-element.28) | copy-start | bytes 6291460
  388.3 2.2 copy-start.22
  389.2 2.2 copy-start.1
  (10 other events, 11.6 us)
Sparse Core Ops, SparseCore 0:
  58.2 9.4 reduce-scatter.2
  100.8 236.3 all-reduce.4
  339.4 7.0 reduce-scatter.4
  349.1 35.5 all-reduce.6
